TPU v7x, 256 devices: a whole 4x4x8 slice. The times are simulated.
256 devices in a mesh: grp: 8 (over x, core), dev: 32 (over y, z).
Axes of the slice: x: 4, y: 4, z: 8, core: 2. Of those that a mesh axis runs over, the one named last changes fastest.
Arguments:
- tensor_slab: bfloat16 [512, 512, 64, 64], P(None, 'dev', 'grp'), may hold values from -400 to 400
- mode_factor: bfloat16 [512, 64], replicated, may hold values from -40 to 40
Outputs:
- triangle: float32 [512, 512], P('dev', 'grp')
All inputs are finite; a program needn't handle non-finite values.
Results may differ from a plain program's by a relative error of at most 0.00033.
Values may be sent and summed in bfloat16 or wider, within the bound.
A program may use at most 64 MiB of HBM per device.

v0:
```python
import jax
import jax.numpy as jnp
from jax import lax
from jax.sharding import PartitionSpec as P


def own_block(full_tri):
    order = full_tri.shape[0]
    row_count = order // lax.axis_size("dev")
    col_count = order // lax.axis_size("grp")
    row_start = lax.axis_index("dev") * row_count
    col_start = lax.axis_index("grp") * col_count
    return lax.dynamic_slice(full_tri, (row_start, col_start), (row_count, col_count))


def per_device(tensor_slab, mode_factor):
    row_width = tensor_slab.shape[0]
    local_cols = tensor_slab.shape[1]
    slab_depth = tensor_slab.shape[2]
    species = tensor_slab.shape[3]
    flat_slab = tensor_slab.reshape(row_width, local_cols * slab_depth * species)
    projected = lax.dot_general(
        mode_factor, flat_slab, (((0,), (0,)), ((), ())), preferred_element_type=jnp.float32
    )
    projected = projected.astype(jnp.bfloat16).reshape(
        mode_factor.shape[1], local_cols, slab_depth * species
    )
    regrouped = lax.all_to_all(projected, "dev", split_axis=0, concat_axis=1, tiled=True)
    gram_local = lax.dot_general(
        regrouped, regrouped, (((0, 2), (0, 2)), ((), ())), preferred_element_type=jnp.float32
    )
    row_total = mode_factor.shape[1] * slab_depth * species * lax.axis_size("grp")
    gram_local = gram_local / row_total
    gram_total = lax.psum(gram_local, ("grp", "dev"))
    return own_block(jnp.linalg.cholesky(gram_total).T)


def solution(mesh):
    in_specs = (P(None, "dev", "grp", None), P())
    out_specs = P("dev", "grp")
    return jax.shard_map(
        per_device, mesh=mesh, in_specs=in_specs, out_specs=out_specs, check_vma=False
    )
```

profile of v0, /device:TPU:2, one launch (start us, length us, event | category | flops | bytes accessed | tf_op | source)
XLA Modules:
  0.0 405.6 jit_solution(6353518399661913828)
XLA Ops:
  6.5 0.0 copy-start
  6.5 0.0 all-reduce.3.cloned.1.call-start
  6.5 0.8 copy-done
  7.4 6.0 %convolution_convert_fusion = bf16[64,8192]{1,0:T(8,128)(2,1)S(1)} fusion(bf16[512,64]{0,1:T(8,128)(2,1)S(1)} %copy-done, bf16[512,8192]{0,1:T(8,128)(2,1)} %bitcast.37), kind=kOutput, calls=%fused_computation | convolution fusion | flops 537395200 | bytes 9502720 | tf_op jit(solution)/shard_map/dot_general | solution.py:22
  13.4 0.4 copy.14
  13.7 39.9 %all_to_all.18 = bf16[64,16,512]{2,1,0:T(8,128)(2,1)S(1)} all-to-all(bf16[64,16,512]{2,1,0:T(8,128)(2,1)S(1)} %bitcast.38), channel_id=1, replica_groups=mesh['grp'=8,'dev'=32] {'dev'}, dimensions={0} | all-to-all | bytes 2097152 | tf_op jit(solution)/shard_map/all_to_all | solution.py:28
  53.6 0.1 copy.3
  53.7 1.8 fusion
  55.5 0.0 all-reduce.3.cloned.1.call-update
  55.5 255.8 %all-reduce.3.cloned.1.call-done = f32[512,512]{0,1:T(8,128)} async-done(((f32[512,512]{0,1:T(8,128)}), f32[512,512]{0,1:T(8,128)}) %all-reduce.3.cloned.1.call-update) | async-done | bytes 1048592 | tf_op jit(solution)/shard_map/psum | solution.py:34
  311.3 1.6 copy.5
  312.9 1.4 fusion.1
  314.4 11.7 %cholesky.104 = f32[128,128]{1,0:T(8,128)S(1)} custom-call(f32[128,128]{1,0:T(8,128)S(1)} %cholesky.266), custom_call_target="Cholesky" | custom-call | tf_op jit(solution)/shard_map/jit(cholesky)/cholesky | solution.py:35
  326.1 9.8 %custom-call.27 = f32[1,128,128]{1,2,0:T(8,128)S(1)} custom-call(f32[1,128,128]{2,1,0:T(8,128)S(1)} %get-tuple-element.14), custom_call_target="InvertDiagBlocksLowerTriangular" | custom-call | tf_op jit(solution)/shard_map/jit(cholesky)/cholesky | solution.py:35
  335.9 0.4 fusion.4
  336.3 0.1 copy.6
  336.5 0.5 convolution_subtract_fusion
  337.0 0.1 cholesky.224
  337.1 11.7 %cholesky.217 = f32[128,128]{1,0:T(8,128)S(1)} custom-call(f32[128,128]{1,0:T(8,128)S(1)} %cholesky.270), custom_call_target="Cholesky" | custom-call | tf_op jit(solution)/shard_map/jit(cholesky)/cholesky | solution.py:35
  348.9 9.9 %custom-call.28 = f32[1,128,128]{1,2,0:T(8,128)S(1)} custom-call(f32[1,128,128]{2,1,0:T(8,128)S(1)} %get-tuple-element.11), custom_call_target="InvertDiagBlocksLowerTriangular" | custom-call | tf_op jit(solution)/shard_map/jit(cholesky)/cholesky | solution.py:35
  358.8 0.3 convolution_dynamic-update-slice_fusion
  359.1 0.4 convolution_subtract_fusion.1
  359.5 11.7 %cholesky.238 = f32[128,128]{1,0:T(8,128)S(1)} custom-call(f32[128,128]{1,0:T(8,128)S(1)} %cholesky.275), custom_call_target="Cholesky" | custom-call | tf_op jit(solution)/shard_map/jit(cholesky)/cholesky | solution.py:35
  371.2 0.7 compare_reduce_fusion.1
  372.0 9.8 %custom-call.29 = f32[1,128,128]{1,2,0:T(8,128)S(1)} custom-call(f32[1,128,128]{2,1,0:T(8,128)S(1)} %get-tuple-element.8), custom_call_target="InvertDiagBlocksLowerTriangular" | custom-call | tf_op jit(solution)/shard_map/jit(cholesky)/cholesky | solution.py:35
  381.8 0.2 convolution_dynamic-update-slice_fusion.1
  382.0 0.4 convolution_subtract_fusion.2
  382.4 11.7 %cholesky.255 = f32[128,128]{1,0:T(8,128)S(1)} custom-call(f32[128,128]{1,0:T(8,128)S(1)} %convolution_subtract_fusion.2), custom_call_target="Cholesky" | custom-call | tf_op jit(solution)/shard_map/jit(cholesky)/cholesky | solution.py:35
  394.1 0.6 compare_reduce_fusion
  394.7 0.7 compare_reduce_fusion.2
  398.0 0.1 fusion.14
  398.0 0.7 copy.9
  (8 shorter events, 0.2 us)
Async XLA Ops:
  6.5 0.8 copy-start
  6.5 304.8 %all-reduce.3.cloned.1.call-start = ((), (), s32[]{:S(2)}) async-start(), calls=%async_computation.1 | async-start | bytes 2097152 | tf_op jit(solution)/shard_map/psum | solution.py:34
Sparse Core Ops, SparseCore 0:
  55.6 255.6 all-reduce.2
where the time goes:
time: 406 us
  waiting for transfers between devices  256 us (63%)
  other arithmetic  80.1 us (20%)
  blocking collectives  39.9 us (10%)
  between operations  16.1 us (4%)
  matrix products  9.9 us (2%)
    psum x1, waiting for transfers between devices, per_device(): gram_total = lax.psum(gram_local, ('grp', 'dev'))  256 us
    another operation x14, other arithmetic, per_device(): return own_block(jnp.linalg.cholesky(gram_total).T)  78.6 us
    all_to_all x1, blocking collectives, per_device(): lax.all_to_all(projected, 'dev', split_axis=0, concat_axis=1, tiled=True)  39.9 us
  transfers between devices with their start and end apart: 1, of which 1 were waited for; matrix products, arithmetic and copies ran while one was open for 0% of the time, Pallas kernels for 0%

commit v1 on v0

--- a/solution.py
+++ b/solution.py
@@ -31,7 +31,7 @@
     )
     row_total = mode_factor.shape[1] * slab_depth * species * lax.axis_size("grp")
     gram_local = gram_local / row_total
-    gram_total = lax.psum(gram_local, ("grp", "dev"))
+    gram_total = lax.psum(lax.psum(gram_local, "dev"), "grp")
     return own_block(jnp.linalg.cholesky(gram_total).T)
 
 

time: 406 us -> 365 us (0.90)
  waiting for transfers between devices: 256 us -> 212 us
    psum x1 -> x2, waiting for transfers between devices: 256 us -> 212 us  [per_device(): gram_total = lax.psum(lax.psum(gram_local, 'dev'), 'grp')]
  transfers between devices with their start and end apart: 1 -> 2, of which waited for: 1 -> 2; matrix products, arithmetic and copies ran while one was open for 0% -> 0% of each run, Pallas kernels for 0% -> 0%
where the time goes in v1:
time: 365 us; the launch traced here: 362 us
  waiting for transfers between devices  212 us (58%)
  other arithmetic  80.1 us (22%)
  blocking collectives  39.9 us (11%)
  between operations  16.1 us (4%)
  matrix products  9.9 us (3%)
  local copies, waits for them, and re-layouts  3.77 us (1%)
    psum x2, waiting for transfers between devices, per_device(): gram_total = lax.psum(lax.psum(gram_local, 'dev'), 'grp')  212 us
    another operation x14, other arithmetic, per_device(): return own_block(jnp.linalg.cholesky(gram_total).T)  78.6 us
    all_to_all x1, blocking collectives, per_device(): lax.all_to_all(projected, 'dev', split_axis=0, concat_axis=1, tiled=True)  39.9 us
  transfers between devices with their start and end apart: 2, of which 2 were waited for; matrix products, arithmetic and copies ran while one was open for 0% of the time, Pallas kernels for 0%

profile of v1, /device:TPU:2, one launch (start us, length us, event | category | flops | bytes accessed | tf_op | source)
XLA Modules:
  0.0 362.1 jit_solution(11102150243860336392)
XLA Ops:
  6.5 0.0 copy-start
  6.5 0.0 all-reduce.4.cloned.1.call-start
  6.5 0.8 copy-done
  7.4 6.0 %convolution_convert_fusion = bf16[64,8192]{1,0:T(8,128)(2,1)S(1)} fusion(bf16[512,64]{0,1:T(8,128)(2,1)S(1)} %copy-done, bf16[512,8192]{0,1:T(8,128)(2,1)} %bitcast.37), kind=kOutput, calls=%fused_computation | convolution fusion | flops 537395200 | bytes 9502720 | tf_op jit(solution)/shard_map/dot_general | solution.py:22
  13.4 0.4 copy.14
  13.7 39.9 %all_to_all.18 = bf16[64,16,512]{2,1,0:T(8,128)(2,1)S(1)} all-to-all(bf16[64,16,512]{2,1,0:T(8,128)(2,1)S(1)} %bitcast.38), channel_id=1, replica_groups=mesh['grp'=8,'dev'=32] {'dev'}, dimensions={0} | all-to-all | bytes 2097152 | tf_op jit(solution)/shard_map/all_to_all | solution.py:28
  53.6 0.1 copy.3
  53.7 1.8 fusion
  55.5 0.0 all-reduce.4.cloned.1.call-update
  55.5 0.2 all-reduce.6.cloned.1.call-start
  55.8 147.0 %all-reduce.4.cloned.1.call-done = f32[512,512]{0,1:T(8,128)} async-done(((f32[512,512]{0,1:T(8,128)}), f32[512,512]{0,1:T(8,128)}) %all-reduce.4.cloned.1.call-update) | async-done | bytes 1048592 | tf_op jit(solution)/shard_map/psum | solution.py:34
  202.8 0.0 all-reduce.6.cloned.1.call-update
  202.8 65.0 %all-reduce.6.cloned.1.call-done = f32[512,512]{0,1:T(8,128)} async-done(((f32[512,512]{0,1:T(8,128)}), f32[512,512]{0,1:T(8,128)}) %all-reduce.6.cloned.1.call-update) | async-done | bytes 1048592 | tf_op jit(solution)/shard_map/psum | solution.py:34
  267.8 1.6 copy.5
  269.4 1.4 fusion.1
  270.9 11.7 %cholesky.104 = f32[128,128]{1,0:T(8,128)S(1)} custom-call(f32[128,128]{1,0:T(8,128)S(1)} %cholesky.266), custom_call_target="Cholesky" | custom-call | tf_op jit(solution)/shard_map/jit(cholesky)/cholesky | solution.py:35
  282.6 9.8 %custom-call.27 = f32[1,128,128]{1,2,0:T(8,128)S(1)} custom-call(f32[1,128,128]{2,1,0:T(8,128)S(1)} %get-tuple-element.14), custom_call_target="InvertDiagBlocksLowerTriangular" | custom-call | tf_op jit(solution)/shard_map/jit(cholesky)/cholesky | solution.py:35
  292.4 0.4 fusion.4
  292.8 0.1 copy.6
  293.0 0.5 convolution_subtract_fusion
  293.5 0.1 cholesky.224
  293.6 11.7 %cholesky.217 = f32[128,128]{1,0:T(8,128)S(1)} custom-call(f32[128,128]{1,0:T(8,128)S(1)} %cholesky.270), custom_call_target="Cholesky" | custom-call | tf_op jit(solution)/shard_map/jit(cholesky)/cholesky | solution.py:35
  305.4 10.0 %custom-call.28 = f32[1,128,128]{1,2,0:T(8,128)S(1)} custom-call(f32[1,128,128]{2,1,0:T(8,128)S(1)} %get-tuple-element.11), custom_call_target="InvertDiagBlocksLowerTriangular" | custom-call | tf_op jit(solution)/shard_map/jit(cholesky)/cholesky | solution.py:35
  315.4 0.3 convolution_dynamic-update-slice_fusion
  315.6 0.4 convolution_subtract_fusion.1
  316.0 11.7 %cholesky.238 = f32[128,128]{1,0:T(8,128)S(1)} custom-call(f32[128,128]{1,0:T(8,128)S(1)} %cholesky.275), custom_call_target="Cholesky" | custom-call | tf_op jit(solution)/shard_map/jit(cholesky)/cholesky | solution.py:35
  327.8 0.7 compare_reduce_fusion.1
  328.5 9.8 %custom-call.29 = f32[1,128,128]{1,2,0:T(8,128)S(1)} custom-call(f32[1,128,128]{2,1,0:T(8,128)S(1)} %get-tuple-element.8), custom_call_target="InvertDiagBlocksLowerTriangular" | custom-call | tf_op jit(solution)/shard_map/jit(cholesky)/cholesky | solution.py:35
  338.3 0.2 convolution_dynamic-update-slice_fusion.1
  338.5 0.4 convolution_subtract_fusion.2
  338.9 11.7 %cholesky.255 = f32[128,128]{1,0:T(8,128)S(1)} custom-call(f32[128,128]{1,0:T(8,128)S(1)} %convolution_subtract_fusion.2), custom_call_target="Cholesky" | custom-call | tf_op jit(solution)/shard_map/jit(cholesky)/cholesky | solution.py:35
  350.7 0.6 compare_reduce_fusion
  351.3 0.7 compare_reduce_fusion.2
  354.5 0.1 fusion.14
  354.6 0.7 copy.9
  (8 shorter events, 0.2 us)
Async XLA Ops:
  6.5 0.8 copy-start
  6.5 196.3 %all-reduce.4.cloned.1.call-start = ((), (), s32[]{:S(2)}) async-start(), calls=%async_computation.1 | async-start | bytes 2097152 | tf_op jit(solution)/shard_map/psum | solution.py:34
  55.5 212.3 %all-reduce.6.cloned.1.call-start = ((), (), s32[]{:S(2)}) async-start(), calls=%async_computation.2 | async-start | bytes 2097152 | tf_op jit(solution)/shard_map/psum | solution.py:34
Sparse Core Ops, SparseCore 0:
  55.6 147.1 all-reduce.3
  205.1 62.6 all-reduce.5
